TPU v7x, 32 devices: a whole 2x2x4 slice. The times are simulated.
32 devices in a mesh: dp: 4 (over y, core), ctx: 4 (over z), tsp: 2 (over x).
Axes of the slice: x: 2, y: 2, z: 4, core: 2. Of those that a mesh axis runs over, the one named last changes fastest.
Arguments:
- grad_out: bfloat16 [4, 1024, 8192], P('dp', 'ctx', 'tsp'), may hold values from -6 to 6
- attn_out: bfloat16 [4, 1024, 4096], P('dp', None, 'ctx'), may hold values from -6 to 6
- out_weight: bfloat16 [4096, 8192], P('ctx', 'tsp'), may hold values from -0.0625 to 0.0625
- query: bfloat16 [4, 1024, 4096], P('dp', 'tsp', 'ctx'), may hold values from -128 to 128
- keys: bfloat16 [4, 1024, 512], P('dp'), may hold values from -128 to 128
- values: bfloat16 [4, 1024, 512], P('dp'), may hold values from -6 to 6
- segment_ids: int32 [4, 1024], P('dp'), may hold values from 0 to 7, never falling along the last dimension, each value on 1 to 256 neighbouring positions
- tile_live: int32 [4, 8, 8], P('dp'), may hold values 0 or 1
Outputs:
- grad_query: bfloat16 [4, 1024, 4096], P('dp', 'tsp', 'ctx')
- grad_keys: bfloat16 [4, 1024, 512], P('dp', ('ctx', 'tsp'))
- grad_values: bfloat16 [4, 1024, 512], P('dp', ('ctx', 'tsp'))
- grad_weight: float32 [4096, 8192], P('ctx', 'tsp')
Inputs may be any that keep to these rules, and one draw needn't show every extreme that they name: `segment_ids`: segment numbers never fall along a row and segment 0 is the source document; each segment has 1 to 256 tokens, one exactly that many.
All inputs are finite; a program needn't handle non-finite values. No bound on the sum of `tile_live` on one device may be relied on, other than what follows from the above.
Results may differ from a plain program's by a relative error of at most 0.0058.
Values may be sent and summed in bfloat16 or wider, within the bound.
A program may use at most 128 MiB of HBM per device.

v0:
```python
import math

import jax
import jax.numpy as jnp
from jax import lax
from jax.sharding import PartitionSpec as P

HEADS = 32
KV_HEADS = 4
HEAD_DIM = 128
TILE = 128


def merge_group(tensor_in):
    row_count = tensor_in.shape[0]
    folded = tensor_in.reshape(row_count, KV_HEADS, HEADS // KV_HEADS, HEAD_DIM).sum(axis=2)
    return folded.reshape(row_count, KV_HEADS * HEAD_DIM)


def per_device(grad_out, attn_out, out_weight, query, keys, values, segment_ids, tile_live):
    score_scale = 1.0 / math.sqrt(HEAD_DIM)
    out_all = attn_out[0]
    seq_len = out_all.shape[0]
    feat_width = out_all.shape[1]
    dy_block = lax.all_gather(grad_out, "ctx", axis=1, tiled=True)[0]
    proj_rows = lax.dot_general(
        dy_block, out_weight, (((1,), (1,)), ((), ())), preferred_element_type=jnp.float32
    )
    grad_part = proj_rows
    weight_part = lax.dot_general(
        out_all, dy_block, (((0,), (0,)), ((), ())), preferred_element_type=jnp.float32
    )
    grad_part, weight_part = (grad_part, weight_part)
    grad_weight = lax.psum(weight_part, "dp")
    out_grad = lax.psum_scatter(grad_part, "tsp", scatter_dimension=0, tiled=True).astype(
        jnp.bfloat16
    )
    quarter = out_grad.shape[0]
    row_start = lax.axis_index("tsp") * quarter
    heads_dev = feat_width // HEAD_DIM
    group_size = HEADS // KV_HEADS
    head_ids = lax.axis_index("ctx") * heads_dev + jnp.arange(heads_dev, dtype=jnp.int32)
    kv_ids = head_ids // group_size
    query_pos = row_start + jnp.arange(quarter, dtype=jnp.int32)
    key_pos = jnp.arange(seq_len, dtype=jnp.int32)
    tile_count = seq_len // TILE
    tile_rows = lax.dynamic_slice_in_dim(tile_live[0], row_start // TILE, quarter // TILE, 0)
    tile_mask = (
        jnp.broadcast_to(
            tile_rows[:, None, :, None], (quarter // TILE, TILE, tile_count, TILE)
        ).reshape(quarter, seq_len)
        == 1
    )
    same_tile = query_pos[:, None] // TILE == key_pos[None, :] // TILE
    segments = segment_ids[0]
    query_seg = lax.dynamic_slice_in_dim(segments, row_start, quarter, 0)
    same_doc = (segments[None, :] == query_seg[:, None]) | (segments[None, :] == 0)
    allowed = (tile_mask | same_tile) & same_doc & (key_pos[None, :] <= query_pos[:, None])

    def split_heads(tensor_in):
        return tensor_in.reshape(tensor_in.shape[0], heads_dev, HEAD_DIM).transpose(1, 0, 2)

    query_heads = split_heads(query[0])
    grad_heads = split_heads(out_grad)
    output_heads = split_heads(lax.dynamic_slice_in_dim(out_all, row_start, quarter, 0))
    key_table = keys[0].reshape(seq_len, KV_HEADS, HEAD_DIM)
    value_table = values[0].reshape(seq_len, KV_HEADS, HEAD_DIM)

    def one_head(head_items):
        query_head, grad_head, output_head, kv_index = head_items
        key_head = lax.dynamic_index_in_dim(key_table, kv_index, 1, keepdims=False)
        value_head = lax.dynamic_index_in_dim(value_table, kv_index, 1, keepdims=False)
        scores = (
            lax.dot_general(
                query_head, key_head, (((1,), (1,)), ((), ())), preferred_element_type=jnp.float32
            )
            * score_scale
        )
        scores = jnp.where(allowed, scores, -jnp.inf)
        row_max = jnp.max(scores, axis=1, keepdims=True)
        lse = row_max + jnp.log(jnp.sum(jnp.exp(scores - row_max), axis=1, keepdims=True))
        probs_f = jnp.where(allowed, jnp.exp(scores - lse), 0.0)
        probs = probs_f.astype(jnp.bfloat16)
        value_term = lax.dot_general(
            probs, grad_head, (((0,), (0,)), ((), ())), preferred_element_type=jnp.float32
        )
        dprobs = lax.dot_general(
            grad_head, value_head, (((1,), (1,)), ((), ())), preferred_element_type=jnp.float32
        )
        delta = jnp.sum(
            grad_head.astype(jnp.float32) * output_head.astype(jnp.float32), axis=1, keepdims=True
        )
        dscores = (probs_f * (dprobs - delta)).astype(jnp.bfloat16)
        query_grad = (
            jnp.dot(dscores, key_head, preferred_element_type=jnp.float32) * score_scale
        ).astype(jnp.bfloat16)
        key_term = (
            lax.dot_general(
                dscores, query_head, (((0,), (0,)), ((), ())), preferred_element_type=jnp.float32
            )
            * score_scale
        )
        return (query_grad, key_term, value_term)

    query_grads, key_terms, value_terms = lax.map(
        one_head, (query_heads, grad_heads, output_heads, kv_ids)
    )
    grad_query = query_grads.transpose(1, 0, 2).reshape(quarter, feat_width)
    key_cols = key_terms.transpose(1, 0, 2).reshape(seq_len, feat_width)
    value_cols = value_terms.transpose(1, 0, 2).reshape(seq_len, feat_width)
    key_recv, value_recv = (
        lax.all_to_all(key_cols, "ctx", split_axis=0, concat_axis=1, tiled=True),
        lax.all_to_all(value_cols, "ctx", split_axis=0, concat_axis=1, tiled=True),
    )
    key_part, value_part = (
        lax.psum_scatter(merge_group(key_recv), "tsp", scatter_dimension=0, tiled=True),
        lax.psum_scatter(merge_group(value_recv), "tsp", scatter_dimension=0, tiled=True),
    )
    grad_keys = key_part.astype(jnp.bfloat16)[None]
    grad_values = value_part.astype(jnp.bfloat16)[None]
    return (grad_query[None], grad_keys, grad_values, grad_weight)


def solution(mesh):
    placed = (
        P("dp", "ctx", "tsp"),
        P("dp", None, "ctx"),
        P("ctx", "tsp"),
        P("dp", "tsp", "ctx"),
        P("dp", None, None),
        P("dp", None, None),
        P("dp", None),
        P("dp", None, None),
    )
    return jax.shard_map(
        per_device,
        mesh=mesh,
        in_specs=placed,
        out_specs=(
            P("dp", "tsp", "ctx"),
            P("dp", ("ctx", "tsp"), None),
            P("dp", ("ctx", "tsp"), None),
            P("ctx", "tsp"),
        ),
        check_vma=False,
    )
```

profile of v0, /device:TPU:0, one launch (start us, length us, event | category | flops | bytes accessed | tf_op | source)
XLA Modules:
  0.0 900.4 jit_solution(15618256980744114519)
XLA Ops:
  8.0 154.0 %all-gather.2.cloned.1.call-done = bf16[1,1024,4096]{2,1,0:T(8,128)(2,1)} async-done(((bf16[1,256,4096]{2,1,0:T(8,128)(2,1)}), bf16[1,1024,4096]{2,1,0:T(8,128)(2,1)}) %all-gather.2.cloned.1.call-update) | async-done | bytes 8388624 | tf_op jit(solution)/shard_map/all_gather | solution.py:25
  161.9 15.1 %fusion.38 = f32[1024,1024]{1,0:T(8,128)} fusion(bf16[1024,4096]{1,0:T(8,128)(2,1)} %param.12, bf16[1,1024,4096]{2,1,0:T(8,128)(2,1)} %all-gather.2.cloned.1.call-done), kind=kOutput, calls=%fused_computation.47 | convolution fusion | flops 8589934592 | bytes 20971520 | tf_op jit(solution)/shard_map/dot_general | solution.py:26
  184.7 45.1 %reduce-scatter.4.cloned.1.call-done = f32[512,1024]{1,0:T(8,128)} async-done(((f32[1024,1024]{1,0:T(8,128)}), f32[512,1024]{1,0:T(8,128)}) %reduce-scatter.4.cloned.1.call-update) | async-done | bytes 2097168 | tf_op jit(solution)/shard_map/reduce_scatter | solution.py:35
  231.5 129.6 %while.15 = (s32[]{:T(128)}, bf16[8,512,128]{2,1,0:T(8,128)(2,1)}, f32[8,1024,128]{2,1,0:T(8,128)}, f32[8,1024,128]{2,1,0:T(8,128)}, bf16[8,512,128]{1,2,0:T(8,1...) while((s32[]{:T(128)}, bf16[8,512,128]{2,1,0:T(8,128)(2,1)}, ...), condition=%wide.region_5.6_spmd.clone, body=%wide.region_1.5_spmd.clone.sunk | while | flops 689437696 | bytes 16977196 | solution.py:105
  238.3 2.7 multiply_convert_fusion.2
  270.8 2.7 multiply_convert_fusion.2
  287.0 2.7 multiply_convert_fusion.2
  319.4 2.7 multiply_convert_fusion.2
  335.6 2.7 multiply_convert_fusion.2
  361.1 6.6 copy.58
  367.7 4.9 all_to_all.27
  372.6 4.9 all-to-all-start.1
  377.5 6.5 copy.56
  384.0 4.9 all_to_all.24
  388.9 81.9 %all-to-all-done.1 = f32[4,256,1024]{2,1,0:T(8,128)} async-done(((f32[4,256,1024]{2,1,0:T(8,128)}), f32[4,256,1024]{2,1,0:T(8,128)}, u32[]{:S(2)}, u32[]{:S(2)}) %all-to-all-start.1) | async-done | bytes 4194336 | tf_op jit(solution)/shard_map/all_to_all | solution.py:113
  470.8 4.9 all-to-all-start
  475.8 5.1 copy.70
  480.9 3.2 reduce_sum.37
  485.2 83.3 %all-to-all-done = f32[4,256,1024]{2,1,0:T(8,128)} async-done(((f32[4,256,1024]{2,1,0:T(8,128)}), f32[4,256,1024]{2,1,0:T(8,128)}, u32[]{:S(2)}, u32[]{:S(2)}) %all-to-all-start) | async-done | bytes 4194336 | tf_op jit(solution)/shard_map/all_to_all | solution.py:112
  568.5 5.2 copy.69
  573.7 3.2 reduce_sum.36
  578.0 15.0 %fusion.36 = f32[1024,4096]{1,0:T(8,128)} fusion(bf16[1,1024,4096]{2,1,0:T(8,128)(2,1)} %all-gather.2.cloned.1.call-done, bf16[1,1024,1024]{2,1,0:T(8,128)(2,1)S(1)} %copy-done), kind=kOutput, calls=%fused_computation.45 | convolution fusion | flops 8589934592 | bytes 27262976 | tf_op jit(solution)/shard_map/dot_general | solution.py:30
  599.7 282.5 %all-reduce.2.cloned.1.call-done = f32[1024,4096]{1,0:T(8,128)} async-done(((f32[1024,4096]{1,0:T(8,128)}), f32[1024,4096]{1,0:T(8,128)}) %all-reduce.2.cloned.1.call-update) | async-done | bytes 16777232 | tf_op jit(solution)/shard_map/psum | solution.py:34
  882.2 11.7 %copy.104 = f32[1024,4096]{1,0:T(8,128)} copy(f32[1024,4096]{1,0:T(8,128)} %all-reduce.2.cloned.1.call-done) | data formatting | bytes 33554432
  (134 shorter events, 119.0 us)
Async XLA Ops:
  7.2 169.9 %copy-start = (bf16[1,1024,1024]{2,1,0:T(8,128)(2,1)S(1)}, bf16[1,1024,1024]{2,1,0:T(8,128)(2,1)}, u32[]{:S(2)}) copy-start(bf16[1,1024,1024]{2,1,0:T(8,128)(2,1)} %param.11) | copy-start | bytes 6291460
  7.2 154.7 %all-gather.2.cloned.1.call-start = ((), (), s32[]{:S(2)}) async-start(), calls=%async_computation.5 | async-start | bytes 10485760 | tf_op jit(solution)/shard_map/all_gather | solution.py:25
  7.9 221.8 %reduce-scatter.4.cloned.1.call-start = ((), (), s32[]{:S(2)}) async-start(), calls=%async_computation.6 | async-start | bytes 6291456 | tf_op jit(solution)/shard_map/reduce_scatter | solution.py:35
  178.5 2.4 copy-start.1
  180.9 3.6 copy-start.3
  180.9 3.7 copy-start.2
  372.6 98.3 %all-to-all-start.1 = ((f32[4,256,1024]{2,1,0:T(8,128)}), f32[4,256,1024]{2,1,0:T(8,128)}, u32[]{:S(2)}, u32[]{:S(2)}) async-start(f32[4,256,1024]{2,1,0:T(8,128)} %all_to_all.27), calls=%async_computation.3 | async-start | bytes 8388608 | tf_op jit(solution)/shard_map/all_to_all | solution.py:113
  470.8 97.7 %all-to-all-start = ((f32[4,256,1024]{2,1,0:T(8,128)}), f32[4,256,1024]{2,1,0:T(8,128)}, u32[]{:S(2)}, u32[]{:S(2)}) async-start(f32[4,256,1024]{2,1,0:T(8,128)} %all_to_all.24), calls=%async_computation.1 | async-start | bytes 8388608 | tf_op jit(solution)/shard_map/all_to_all | solution.py:112
  475.8 120.4 %reduce-scatter.8.cloned.1.call-start = ((), (), s32[]{:S(2)}) async-start(), calls=%async_computation.8 | async-start | bytes 786432 | tf_op jit(solution)/shard_map/reduce_scatter | solution.py:117
  485.1 112.8 %reduce-scatter.6.cloned.1.call-start = ((), (), s32[]{:S(2)}) async-start(), calls=%async_computation.7 | async-start | bytes 786432 | tf_op jit(solution)/shard_map/reduce_scatter | solution.py:116
  578.0 304.2 %all-reduce.2.cloned.1.call-start = ((), (), s32[]{:S(2)}) async-start(), calls=%async_computation.9 | async-start | bytes 33554432 | tf_op jit(solution)/shard_map/psum | solution.py:34
Sparse Core Ops, SparseCore 0:
  9.6 152.3 all-gather.1
  177.1 52.5 reduce-scatter.3
  485.3 15.0 reduce-scatter.7
  578.1 12.7 reduce-scatter.5
  593.8 288.3 all-reduce.1
where the time goes:
time: 902 us; the launch traced here: 900 us
  waiting for transfers between devices  648 us (72%)
  matrix products  124 us (14%)
  local copies, waits for them, and re-layouts  73.7 us (8%)
  loops' own time  15.8 us (2%)
  other arithmetic  15.5 us (2%)
  between operations  13.9 us (2%)
  starting transfers between devices  10.1 us (1%)
    psum x1, waiting for transfers between devices, per_device(): grad_weight = lax.psum(weight_part, 'dp')  282 us
    all_gather x1, waiting for transfers between devices, per_device(): dy_block = lax.all_gather(grad_out, 'ctx', axis=1, tiled=True)[0]  154 us
    all_to_all x1, waiting for transfers between devices, per_device(): lax.all_to_all(key_cols, 'ctx', split_axis=0, concat_axis=1, tiled=True)  83.3 us
    all_to_all x1, waiting for transfers between devices, per_device(): lax.all_to_all(value_cols, 'ctx', split_axis=0, concat_axis=1, tiled=True)  81.9 us
    reduce_scatter x1, waiting for transfers between devices, per_device(): lax.psum_scatter(grad_part, 'tsp', scatter_dimension=0, tiled=True)  45.1 us
    unnamed x17, local copies, waits for them, and re-layouts  31 us
    dot_general x8, matrix products, one_head(): lax.dot_general(grad_head, value_head, (((1,), (1,)), ((), ())), preferre...  21.9 us
    dot_general x8, matrix products, one_head(): lax.dot_general(probs, grad_head, (((0,), (0,)), ((), ())), preferred_ele...  19.1 us
  transfers between devices with their start and end apart: 7, of which 5 were waited for; matrix products, arithmetic and copies ran while one was open for 6% of the time, Pallas kernels for 0%

commit v1 on v0

--- a/solution.py
+++ b/solution.py
@@ -31,7 +31,10 @@
         out_all, dy_block, (((0,), (0,)), ((), ())), preferred_element_type=jnp.float32
     )
     grad_part, weight_part = (grad_part, weight_part)
-    grad_weight = lax.psum(weight_part, "dp")
+    weight_quarter = lax.psum_scatter(weight_part, "dp", scatter_dimension=0, tiled=True)
+    grad_weight = lax.all_gather(
+        weight_quarter.astype(jnp.bfloat16), "dp", axis=0, tiled=True
+    ).astype(jnp.float32)
     out_grad = lax.psum_scatter(grad_part, "tsp", scatter_dimension=0, tiled=True).astype(
         jnp.bfloat16
     )
@@ -106,16 +109,23 @@
         one_head, (query_heads, grad_heads, output_heads, kv_ids)
     )
     grad_query = query_grads.transpose(1, 0, 2).reshape(quarter, feat_width)
-    key_cols = key_terms.transpose(1, 0, 2).reshape(seq_len, feat_width)
-    value_cols = value_terms.transpose(1, 0, 2).reshape(seq_len, feat_width)
-    key_recv, value_recv = (
-        lax.all_to_all(key_cols, "ctx", split_axis=0, concat_axis=1, tiled=True),
-        lax.all_to_all(value_cols, "ctx", split_axis=0, concat_axis=1, tiled=True),
+    local_groups = max(1, heads_dev // group_size)
+
+    def fold_local(terms):
+        folded = terms.reshape(local_groups, heads_dev // local_groups, seq_len, HEAD_DIM).sum(axis=1)
+        return folded.transpose(1, 0, 2).reshape(seq_len, local_groups * HEAD_DIM)
+
+    def fold_remote(recv):
+        spread = recv.shape[1] // (KV_HEADS * HEAD_DIM)
+        folded = recv.reshape(recv.shape[0], KV_HEADS, spread, HEAD_DIM).sum(axis=2)
+        return folded.reshape(recv.shape[0], KV_HEADS * HEAD_DIM)
+
+    key_recv = lax.all_to_all(fold_local(key_terms), "ctx", split_axis=0, concat_axis=1, tiled=True)
+    value_recv = lax.all_to_all(
+        fold_local(value_terms), "ctx", split_axis=0, concat_axis=1, tiled=True
     )
-    key_part, value_part = (
-        lax.psum_scatter(merge_group(key_recv), "tsp", scatter_dimension=0, tiled=True),
-        lax.psum_scatter(merge_group(value_recv), "tsp", scatter_dimension=0, tiled=True),
-    )
+    key_part = lax.psum_scatter(fold_remote(key_recv), "tsp", scatter_dimension=0, tiled=True)
+    value_part = lax.psum_scatter(fold_remote(value_recv), "tsp", scatter_dimension=0, tiled=True)
     grad_keys = key_part.astype(jnp.bfloat16)[None]
     grad_values = value_part.astype(jnp.bfloat16)[None]
     return (grad_query[None], grad_keys, grad_values, grad_weight)

time: 902 us -> 498 us (0.55)
  waiting for transfers between devices: 648 us -> 249 us
  local copies, waits for them, and re-layouts: 73.7 us -> 27 us
  blocking collectives: 0 us -> 35.3 us
  other arithmetic: 15.5 us -> 29.8 us
  starting transfers between devices: 10.1 us -> 0.42 us
    psum x1 -> x0, waiting for transfers between devices: 282 us -> none  [per_device(): grad_weight = lax.psum(weight_part, 'dp')]
    all_to_all x2 -> x0, waiting for transfers between devices: 165 us -> none  [the longest x1 83.3 us: per_device(): lax.all_to_all(key_cols, 'ctx', split_axis=0, concat_axis=1, tiled=True)]
    all_gather x0 -> x1, waiting for transfers between devices: none -> 58.6 us  [per_device(): lax.all_gather(weight_quarter.astype(jnp.bfloat16), 'dp', axis=0, tiled=T...]
    all_to_all x0 -> x2, blocking collectives: none -> 35.3 us  [the longest x1 18.7 us: per_device(): lax.all_to_all(fold_local(value_terms), 'ctx', split_axis=0, concat_axis=...]
    unnamed x17 -> x22, local copies, waits for them, and re-layouts: 31 us -> 8.16 us
    convert_element_type x0 -> x2, other arithmetic: none -> 15.8 us  [the longest x1 12 us: per_device(): grad_weight = lax.all_gather(weight_quarter.astype(jnp.bfloat16), 'dp', a...]
    transpose x2 -> x0, local copies, waits for them, and re-layouts: 13.1 us -> none  [the longest x1 6.57 us: per_device(): value_cols = value_terms.transpose(1, 0, 2).reshape(seq_len, feat_width)]
    reduce_scatter x1, waiting for transfers between devices: 45.1 us -> 32 us  [per_device(): lax.psum_scatter(grad_part, 'tsp', scatter_dimension=0, tiled=True)]
  transfers between devices with their start and end apart: 7 -> 6, of which waited for: 5 -> 4; matrix products, arithmetic and copies ran while one was open for 6% -> 31% of each run, Pallas kernels for 0% -> 0%
where the time goes in v1:
time: 498 us; the launch traced here: 496 us
  waiting for transfers between devices  249 us (50%)
  matrix products  124 us (25%)
  blocking collectives  35.3 us (7%)
  other arithmetic  29.8 us (6%)
  local copies, waits for them, and re-layouts  27 us (5%)
  loops' own time  15.8 us (3%)
  between operations  14.3 us (3%)
    all_gather x1, waiting for transfers between devices, per_device(): dy_block = lax.all_gather(grad_out, 'ctx', axis=1, tiled=True)[0]  154 us
    all_gather x1, waiting for transfers between devices, per_device(): lax.all_gather(weight_quarter.astype(jnp.bfloat16), 'dp', axis=0, tiled=T...  58.6 us
    reduce_scatter x1, waiting for transfers between devices, per_device(): lax.psum_scatter(grad_part, 'tsp', scatter_dimension=0, tiled=True)  32 us
    dot_general x8, matrix products, one_head(): lax.dot_general(grad_head, value_head, (((1,), (1,)), ((), ())), preferre...  22 us
    dot_general x8, matrix products, one_head(): lax.dot_general(query_head, key_head, (((1,), (1,)), ((), ())), preferred...  19 us
    dot_general x8, matrix products, one_head(): lax.dot_general(probs, grad_head, (((0,), (0,)), ((), ())), preferred_ele...  18.9 us
    all_to_all x1, blocking collectives, per_device(): lax.all_to_all(fold_local(value_terms), 'ctx', split_axis=0, concat_axis=...  18.7 us
    dot_general x8, matrix products, one_head(): lax.dot_general(dscores, query_head, (((0,), (0,)), ((), ())), preferred_...  17.5 us
  transfers between devices with their start and end apart: 6, of which 4 were waited for; matrix products, arithmetic and copies ran while one was open for 31% of the time, Pallas kernels for 0%

profile of v1, /device:TPU:0, one launch (start us, length us, event | category | flops | bytes accessed | tf_op | source)
XLA Modules:
  0.0 495.9 jit_solution(4312816865522546725)
XLA Ops:
  8.0 154.0 %all-gather.3.cloned.1.call-done = bf16[1,1024,4096]{2,1,0:T(8,128)(2,1)} async-done(((bf16[1,256,4096]{2,1,0:T(8,128)(2,1)}), bf16[1,1024,4096]{2,1,0:T(8,128)(2,1)}) %all-gather.3.cloned.1.call-update) | async-done | bytes 8388624 | tf_op jit(solution)/shard_map/all_gather | solution.py:25
  161.9 15.1 %fusion.38 = f32[1024,1024]{1,0:T(8,128)} fusion(bf16[1024,4096]{1,0:T(8,128)(2,1)} %param.12, bf16[1,1024,4096]{2,1,0:T(8,128)(2,1)} %all-gather.3.cloned.1.call-done), kind=kOutput, calls=%fused_computation.47 | convolution fusion | flops 8589934592 | bytes 20971520 | tf_op jit(solution)/shard_map/dot_general | solution.py:26
  177.1 14.8 %fusion.36 = f32[1024,4096]{1,0:T(8,128)} fusion(bf16[1,1024,4096]{2,1,0:T(8,128)(2,1)} %all-gather.3.cloned.1.call-done, bf16[1,1024,1024]{2,1,0:T(8,128)(2,1)S(1)} %copy-done), kind=kOutput, calls=%fused_computation.45 | convolution fusion | flops 8589934592 | bytes 27262976 | tf_op jit(solution)/shard_map/dot_general | solution.py:30
  197.8 32.0 %reduce-scatter.5.cloned.1.call-done = f32[512,1024]{1,0:T(8,128)} async-done(((f32[1024,1024]{1,0:T(8,128)}), f32[512,1024]{1,0:T(8,128)}) %reduce-scatter.5.cloned.1.call-update) | async-done | bytes 2097168 | tf_op jit(solution)/shard_map/reduce_scatter | solution.py:38
  231.5 129.9 %while.15 = (s32[]{:T(128)}, bf16[8,512,128]{2,1,0:T(8,128)(2,1)}, f32[8,1024,128]{2,1,0:T(8,128)}, f32[8,1024,128]{2,1,0:T(8,128)}, bf16[8,512,128]{1,2,0:T(8,1...) while((s32[]{:T(128)}, bf16[8,512,128]{2,1,0:T(8,128)(2,1)}, ...), condition=%wide.region_5.6_spmd.clone, body=%wide.region_1.5_spmd.clone.sunk | while | flops 689437696 | bytes 16977196 | solution.py:108
  238.3 2.8 multiply_convert_fusion.2
  251.9 2.5 fusion.73
  254.9 2.8 multiply_convert_fusion.2
  259.7 2.4 fusion.77
  271.2 2.7 multiply_convert_fusion.2
  284.5 2.4 fusion.73
  287.4 2.7 multiply_convert_fusion.2
  303.6 2.7 multiply_convert_fusion.2
  319.7 2.7 multiply_convert_fusion.2
  335.9 2.7 multiply_convert_fusion.2
  352.0 2.7 multiply_convert_fusion.2
  361.4 2.4 reduce_sum.38
  363.8 18.7 %all_to_all.32 = f32[4,256,128]{2,1,0:T(8,128)S(1)} all-to-all(f32[4,256,128]{2,1,0:T(8,128)S(1)} %bitcast.140), channel_id=1, replica_groups=mesh['dp'=4,'ctx'=4,'tsp'=2] {'ctx'}, dimensions={0} | all-to-all | bytes 1048576 | tf_op jit(solution)/shard_map/all_to_all | solution.py:124
  383.7 2.4 reduce_sum.37
  386.2 16.6 %all_to_all.33 = f32[4,256,128]{2,1,0:T(8,128)S(1)} all-to-all(f32[4,256,128]{2,1,0:T(8,128)S(1)} %bitcast.139), channel_id=1, replica_groups=mesh['dp'=4,'ctx'=4,'tsp'=2] {'ctx'}, dimensions={0} | all-to-all | bytes 1048576 | tf_op jit(solution)/shard_map/all_to_all | solution.py:123
  403.9 3.8 convert_element_type.36
  412.7 4.2 reduce-scatter.7.cloned.1.call-done
  418.6 58.6 %all-gather.5.cloned.1.call-done = bf16[1024,4096]{1,0:T(8,128)(2,1)} async-done(((bf16[256,4096]{1,0:T(8,128)(2,1)}), bf16[1024,4096]{1,0:T(8,128)(2,1)}) %all-gather.5.cloned.1.call-update) | async-done | bytes 8388624 | tf_op jit(solution)/shard_map/all_gather | solution.py:35
  477.1 12.0 %convert_element_type.37 = f32[1024,4096]{1,0:T(8,128)} convert(bf16[1024,4096]{1,0:T(8,128)(2,1)} %all-gather.5.cloned.1.call-done) | non-fusion elementwise | flops 4194304 | bytes 25165824 | tf_op jit(solution)/shard_map/convert_element_type | solution.py:37
  (138 shorter events, 102.1 us)
Async XLA Ops:
  7.2 169.9 %copy-start = (bf16[1,1024,1024]{2,1,0:T(8,128)(2,1)S(1)}, bf16[1,1024,1024]{2,1,0:T(8,128)(2,1)}, u32[]{:S(2)}) copy-start(bf16[1,1024,1024]{2,1,0:T(8,128)(2,1)} %param.11) | copy-start | bytes 6291460
  7.2 154.7 %all-gather.3.cloned.1.call-start = ((), (), s32[]{:S(2)}) async-start(), calls=%async_computation.6 | async-start | bytes 10485760 | tf_op jit(solution)/shard_map/all_gather | solution.py:25
  7.9 221.8 %reduce-scatter.5.cloned.1.call-start = ((), (), s32[]{:S(2)}) async-start(), calls=%async_computation.7 | async-start | bytes 6291456 | tf_op jit(solution)/shard_map/reduce_scatter | solution.py:38
  177.0 226.9 %reduce-scatter.11.cloned.1.call-start = ((), (), s32[]{:S(2)}) async-start(), calls=%async_computation.10 | async-start | bytes 20971520 | tf_op jit(solution)/shard_map/reduce_scatter | solution.py:34
  191.9 219.1 %reduce-scatter.9.cloned.1.call-start = ((), (), s32[]{:S(2)}) async-start(), calls=%async_computation.9 | async-start | bytes 786432 | tf_op jit(solution)/shard_map/reduce_scatter | solution.py:128
  192.2 1.4 copy-start.2
  192.2 2.7 copy-start.3
  193.6 2.7 copy-start.4
  195.0 2.7 copy-start.7
  195.0 2.7 copy-start.6
  383.7 33.2 %reduce-scatter.7.cloned.1.call-start = ((), (), s32[]{:S(2)}) async-start(), calls=%async_computation.8 | async-start | bytes 786432 | tf_op jit(solution)/shard_map/reduce_scatter | solution.py:127
  403.9 73.3 %all-gather.5.cloned.1.call-start = ((), (), s32[]{:S(2)}) async-start(), calls=%async_computation.11 | async-start | bytes 10485760 | tf_op jit(solution)/shard_map/all_gather | solution.py:35
  407.7 1.2 copy-start.5
  477.1 12.0 %copy-start.1 = (bf16[1,1024,1024]{2,1,0:T(8,128)(2,1)S(1)}, bf16[1,1024,1024]{2,1,0:T(8,128)(2,1)}, u32[]{:S(2)}) copy-start(bf16[1,1024,1024]{2,1,0:T(8,128)(2,1)} %param.11) | copy-start | bytes 6291460
Sparse Core Ops, SparseCore 0:
  9.6 152.3 all-gather.2
  177.1 52.5 reduce-scatter.4
  232.9 125.0 reduce-scatter.10
  383.8 12.8 reduce-scatter.8
  404.0 12.8 reduce-scatter.6
  418.8 58.2 all-gather.4

commit v2 on v1

--- a/solution.py
+++ b/solution.py
@@ -60,55 +60,38 @@
     same_doc = (segments[None, :] == query_seg[:, None]) | (segments[None, :] == 0)
     allowed = (tile_mask | same_tile) & same_doc & (key_pos[None, :] <= query_pos[:, None])
 
-    def split_heads(tensor_in):
-        return tensor_in.reshape(tensor_in.shape[0], heads_dev, HEAD_DIM).transpose(1, 0, 2)
-
-    query_heads = split_heads(query[0])
-    grad_heads = split_heads(out_grad)
-    output_heads = split_heads(lax.dynamic_slice_in_dim(out_all, row_start, quarter, 0))
-    key_table = keys[0].reshape(seq_len, KV_HEADS, HEAD_DIM)
-    value_table = values[0].reshape(seq_len, KV_HEADS, HEAD_DIM)
-
-    def one_head(head_items):
-        query_head, grad_head, output_head, kv_index = head_items
-        key_head = lax.dynamic_index_in_dim(key_table, kv_index, 1, keepdims=False)
-        value_head = lax.dynamic_index_in_dim(value_table, kv_index, 1, keepdims=False)
-        scores = (
-            lax.dot_general(
-                query_head, key_head, (((1,), (1,)), ((), ())), preferred_element_type=jnp.float32
-            )
-            * score_scale
-        )
-        scores = jnp.where(allowed, scores, -jnp.inf)
-        row_max = jnp.max(scores, axis=1, keepdims=True)
-        lse = row_max + jnp.log(jnp.sum(jnp.exp(scores - row_max), axis=1, keepdims=True))
-        probs_f = jnp.where(allowed, jnp.exp(scores - lse), 0.0)
-        probs = probs_f.astype(jnp.bfloat16)
-        value_term = lax.dot_general(
-            probs, grad_head, (((0,), (0,)), ((), ())), preferred_element_type=jnp.float32
-        )
-        dprobs = lax.dot_general(
-            grad_head, value_head, (((1,), (1,)), ((), ())), preferred_element_type=jnp.float32
-        )
-        delta = jnp.sum(
-            grad_head.astype(jnp.float32) * output_head.astype(jnp.float32), axis=1, keepdims=True
-        )
-        dscores = (probs_f * (dprobs - delta)).astype(jnp.bfloat16)
-        query_grad = (
-            jnp.dot(dscores, key_head, preferred_element_type=jnp.float32) * score_scale
-        ).astype(jnp.bfloat16)
-        key_term = (
-            lax.dot_general(
-                dscores, query_head, (((0,), (0,)), ((), ())), preferred_element_type=jnp.float32
-            )
-            * score_scale
-        )
-        return (query_grad, key_term, value_term)
-
-    query_grads, key_terms, value_terms = lax.map(
-        one_head, (query_heads, grad_heads, output_heads, kv_ids)
+    query_heads = query[0].reshape(quarter, heads_dev, HEAD_DIM)
+    grad_heads = out_grad.reshape(quarter, heads_dev, HEAD_DIM)
+    output_heads = lax.dynamic_slice_in_dim(out_all, row_start, quarter, 0).reshape(
+        quarter, heads_dev, HEAD_DIM
     )
-    grad_query = query_grads.transpose(1, 0, 2).reshape(quarter, feat_width)
+    key_heads = jnp.take(keys[0].reshape(seq_len, KV_HEADS, HEAD_DIM), kv_ids, axis=1)
+    value_heads = jnp.take(values[0].reshape(seq_len, KV_HEADS, HEAD_DIM), kv_ids, axis=1)
+    scores = (
+        jnp.einsum("qhd,khd->hqk", query_heads, key_heads, preferred_element_type=jnp.float32)
+        * score_scale
+    )
+    scores = jnp.where(allowed[None], scores, -jnp.inf)
+    row_max = jnp.max(scores, axis=2, keepdims=True)
+    lse = row_max + jnp.log(jnp.sum(jnp.exp(scores - row_max), axis=2, keepdims=True))
+    probs_f = jnp.where(allowed[None], jnp.exp(scores - lse), 0.0)
+    probs = probs_f.astype(jnp.bfloat16)
+    value_terms = jnp.einsum(
+        "hqk,qhd->hkd", probs, grad_heads, preferred_element_type=jnp.float32
+    )
+    dprobs = jnp.einsum("qhd,khd->hqk", grad_heads, value_heads, preferred_element_type=jnp.float32)
+    delta = jnp.sum(
+        grad_heads.astype(jnp.float32) * output_heads.astype(jnp.float32), axis=2
+    ).T[:, :, None]
+    dscores = (probs_f * (dprobs - delta)).astype(jnp.bfloat16)
+    grad_query = (
+        jnp.einsum("hqk,khd->qhd", dscores, key_heads, preferred_element_type=jnp.float32)
+        * score_scale
+    ).astype(jnp.bfloat16).reshape(quarter, feat_width)
+    key_terms = (
+        jnp.einsum("hqk,qhd->hkd", dscores, query_heads, preferred_element_type=jnp.float32)
+        * score_scale
+    )
     local_groups = max(1, heads_dev // group_size)
 
     def fold_local(terms):

time: 498 us -> 471 us (0.946)
  matrix products: 124 us -> 65.4 us
  waiting for transfers between devices: 249 us -> 303 us
  blocking collectives: 35.3 us -> 16.5 us
  other arithmetic: 29.8 us -> 46.1 us
  loops' own time: 15.8 us -> 0 us
  local copies, waits for them, and re-layouts: 27 us -> 19.8 us
    reduce_scatter x1, waiting for transfers between devices: 0.02 us -> 63 us  [per_device(): lax.psum_scatter(weight_part, 'dp', scatter_dimension=0, tiled=True)]
    dot_general x40 -> x5, matrix products: 93.9 us -> 35.6 us  [the longest x1 11.7 us: per_device(): jnp.einsum('qhd,khd->hqk', grad_heads, value_heads, preferred_element_typ...]
    reduce_scatter x1, waiting for transfers between devices: 32 us -> 1.86 us  [per_device(): lax.psum_scatter(grad_part, 'tsp', scatter_dimension=0, tiled=True)]
    all_to_all x1 -> x0, blocking collectives: 16.6 us -> none  [per_device(): lax.all_to_all(fold_local(key_terms), 'ctx', split_axis=0, concat_axis=1,...]
    another operation x1 -> x0, loops' own time: 15.8 us -> none  [per_device(): lax.map(one_head, (query_heads, grad_heads, output_heads, kv_ids))]
    reduce_scatter x1, waiting for transfers between devices: 0.01 us -> 15.1 us  [per_device(): lax.psum_scatter(fold_remote(value_recv), 'tsp', scatter_dimension=0, til...]
    dynamic_slice x25 -> x0, local copies, waits for them, and re-layouts: 13.1 us -> none  [the longest x24 13 us: per_device(): lax.map(one_head, (query_heads, grad_heads, output_heads, kv_ids))]
    convert_element_type x0 -> x1, other arithmetic: none -> 10.8 us  [per_device(): probs = probs_f.astype(jnp.bfloat16)]
  transfers between devices with their start and end apart: 6 -> 7, of which waited for: 4 -> 7; matrix products, arithmetic and copies ran while one was open for 31% -> 21% of each run, Pallas kernels for 0% -> 0%
where the time goes in v2:
time: 471 us; the launch traced here: 470 us
  waiting for transfers between devices  303 us (64%)
  matrix products  65.4 us (14%)
  other arithmetic  46.1 us (10%)
  local copies, waits for them, and re-layouts  19.8 us (4%)
  blocking collectives  16.5 us (4%)
  between operations  14.4 us (3%)
  starting transfers between devices  4.88 us (1%)
    all_gather x1, waiting for transfers between devices, per_device(): dy_block = lax.all_gather(grad_out, 'ctx', axis=1, tiled=True)[0]  154 us
    reduce_scatter x1, waiting for transfers between devices, per_device(): lax.psum_scatter(weight_part, 'dp', scatter_dimension=0, tiled=True)  63 us
    all_gather x1, waiting for transfers between devices, per_device(): lax.all_gather(weight_quarter.astype(jnp.bfloat16), 'dp', axis=0, tiled=T...  58.6 us
    all_to_all x1, blocking collectives, per_device(): lax.all_to_all(fold_local(value_terms), 'ctx', split_axis=0, concat_axis=...  16.5 us
    dot_general x1, matrix products, per_device(): lax.dot_general(dy_block, out_weight, (((1,), (1,)), ((), ())), preferred...  15.1 us
    reduce_scatter x1, waiting for transfers between devices, per_device(): lax.psum_scatter(fold_remote(value_recv), 'tsp', scatter_dimension=0, til...  15.1 us
    dot_general x1, matrix products, per_device(): lax.dot_general(out_all, dy_block, (((0,), (0,)), ((), ())), preferred_el...  14.6 us
    convert_element_type x1, other arithmetic, per_device(): grad_weight = lax.all_gather(weight_quarter.astype(jnp.bfloat16), 'dp', a...  11.8 us
  transfers between devices with their start and end apart: 7, of which 7 were waited for; matrix products, arithmetic and copies ran while one was open for 21% of the time, Pallas kernels for 0%

profile of v2, /device:TPU:0, one launch (start us, length us, event | category | flops | bytes accessed | tf_op | source)
XLA Modules:
  0.0 470.0 jit_solution(11098206023475885056)
XLA Ops:
  8.0 154.0 %all-gather.3.cloned.1.call-done = bf16[1,1024,4096]{2,1,0:T(8,128)(2,1)} async-done(((bf16[1,256,4096]{2,1,0:T(8,128)(2,1)}), bf16[1,1024,4096]{2,1,0:T(8,128)(2,1)}) %all-gather.3.cloned.1.call-update) | async-done | bytes 8388624 | tf_op jit(solution)/shard_map/all_gather | solution.py:25
  161.9 15.1 %fusion.6 = f32[1024,1024]{1,0:T(8,128)} fusion(bf16[1024,4096]{1,0:T(8,128)(2,1)} %param.12, bf16[1,1024,4096]{2,1,0:T(8,128)(2,1)} %all-gather.3.cloned.1.call-done), kind=kOutput, calls=%fused_computation.12 | convolution fusion | flops 8589934592 | bytes 20971520 | tf_op jit(solution)/shard_map/dot_general | solution.py:26
  177.3 14.6 %fusion.4 = f32[1024,4096]{1,0:T(8,128)} fusion(bf16[1,1024,4096]{2,1,0:T(8,128)(2,1)} %all-gather.3.cloned.1.call-done, bf16[1,1024,1024]{2,1,0:T(8,128)(2,1)S(1)} %copy-done.10), kind=kOutput, calls=%fused_computation.10 | convolution fusion | flops 8589934592 | bytes 27262976 | tf_op jit(solution)/shard_map/dot_general | solution.py:30
  201.2 2.1 gather_fusion
  203.4 2.1 gather_fusion.1
  207.5 9.4 %fusion.3 = (f32[8,512]{1,0:T(8,128)S(1)}, f32[8,1024,512]{2,1,0:T(8,128)}) fusion(pred[512,1024]{0,1:T(8,128)(4,1)S(1)} %fusion.16, bf16[512,8,128]{2,1,0:T(8,128)(2,1)S(1)} %bitcast.107, bf16[8,1024,128]{2,1,0:T(8,128)(2,1)} %gather_fusion, pred[8]{0:T(512)(128)(4,1)S(1)} %compare_and_fusion), kind=kOutput, calls=%fused_computation.9 | convolution fusion | flops 1087369216 | bytes 20463624 | tf_op jit(solution)/shard_map/qhd,khd->hqk/dot_general | solution.py:71
  216.9 9.4 %exponential_reduce_fusion = f32[8,512]{1,0:T(8,128)S(1)} fusion(f32[8,1024,512]{2,1,0:T(8,128)} %get-tuple-element.24, f32[8,512]{1,0:T(8,128)S(1)} %get-tuple-element.23, pred[512,1024]{0,1:T(8,128)(4,1)S(1)} %fusion.16), kind=kLoop, calls=%fused_computation.8 | loop fusion | flops 16773120 | bytes 17334272 | tf_op jit(solution)/shard_map/reduce_sum | solution.py:76
  227.9 1.9 reduce-scatter.5.cloned.1.call-done
  229.8 2.9 convert_bitcast_fusion.1
  234.1 11.7 %multiply_convert_fusion = bf16[8,512,1024]{1,2,0:T(8,128)(2,1)S(1)} fusion(f32[8,1024,512]{2,1,0:T(8,128)} %get-tuple-element.24, f32[8,512]{1,0:T(8,128)S(1)} %copy.58, f32[8,512]{1,0:T(8,128)S(1)} %log_add_fusion, pred[512,1024]{0,1:T(8,128)(4,1)S(1)} %copy-done.4, bf16[8,1024,128]{2,1,0:T(8,128)(2,1)} %gather_fusion.1, ...), kind=kOutput, calls=%fused_computation.7 | convolution fusion | flops 1104150528 | bytes 28868616 | tf_op jit(solution)/shard_map/qhd,khd->hqk/dot_general | solution.py:82
  245.8 3.6 multiply_reduce_fusion
  249.4 2.0 copy-done.13
  251.4 4.2 all-to-all-start
  255.7 10.8 %fusion.2 = bf16[1024,512,8]{1,0,2:T(8,128)(2,1)} fusion(f32[8,1024,512]{2,1,0:T(8,128)} %get-tuple-element.24, f32[512,8]{0,1:T(8,128)S(1)} %bitcast.111, pred[1024,512]{1,0:T(8,128)(4,1)S(1)} %fusion.40), kind=kLoop, calls=%fused_computation.5 | loop fusion | flops 20971520 | bytes 25706496 | tf_op jit(solution)/shard_map/convert_element_type | solution.py:78
  266.4 3.1 all-to-all-done
  270.9 5.9 %convolution_bitcast_fusion = f32[4,256,128]{2,1,0:T(8,128)S(1)} fusion(bf16[4,256,512,8]{2,1,0,3:T(8,128)(2,1)} %bitcast.95, bf16[512,8,128,1]{2,1,0,3:T(8,128)(2,1)S(1)} %bitcast.99), kind=kOutput, calls=%fused_computation.31 | convolution fusion | flops 1073741824 | bytes 9961472 | tf_op jit(solution)/shard_map/hqk,qhd->hkd/dot_general | solution.py:79
  276.8 16.5 %all_to_all.29 = f32[4,256,128]{2,1,0:T(8,128)S(1)} all-to-all(f32[4,256,128]{2,1,0:T(8,128)S(1)} %convolution_bitcast_fusion), channel_id=1, replica_groups=mesh['dp'=4,'ctx'=4,'tsp'=2] {'ctx'}, dimensions={0} | all-to-all | bytes 1048576 | tf_op jit(solution)/shard_map/all_to_all | solution.py:107
  294.4 63.0 %reduce-scatter.11.cloned.1.call-done = f32[256,4096]{1,0:T(8,128)} async-done(((f32[1024,4096]{1,0:T(8,128)}), f32[256,4096]{1,0:T(8,128)}) %reduce-scatter.11.cloned.1.call-update) | async-done | bytes 4194320 | tf_op jit(solution)/shard_map/reduce_scatter | solution.py:34
  357.4 3.8 convert_element_type.47
  361.3 5.0 %multiply_convert_fusion.1 = bf16[8,128,512]{2,1,0:T(8,128)(2,1)S(1)} fusion(bf16[8,512,1024]{1,2,0:T(8,128)(2,1)} %copy-done.13, bf16[8,1024,128]{2,1,0:T(8,128)(2,1)S(1)} %copy-done.5, pred[8]{0:T(512)(128)(4,1)S(1)} %compare_and_fusion), kind=kOutput, calls=%fused_computation.23 | convolution fusion | flops 1075838976 | bytes 11534344 | tf_op jit(solution)/shard_map/hqk,khd->qhd/dot_general | solution.py:88
  367.6 6.6 %reduce-scatter.7.cloned.1.call-done = f32[128,512]{0,1:T(8,128)} async-done(((f32[256,512]{0,1:T(8,128)}), f32[128,512]{0,1:T(8,128)}) %reduce-scatter.7.cloned.1.call-update) | async-done | bytes 262160 | tf_op jit(solution)/shard_map/reduce_scatter | solution.py:110
  375.9 15.1 %reduce-scatter.9.cloned.1.call-done = f32[128,512]{0,1:T(8,128)} async-done(((f32[256,512]{0,1:T(8,128)}), f32[128,512]{0,1:T(8,128)}) %reduce-scatter.9.cloned.1.call-update) | async-done | bytes 262160 | tf_op jit(solution)/shard_map/reduce_scatter | solution.py:111
  392.7 58.6 %all-gather.5.cloned.1.call-done = bf16[1024,4096]{1,0:T(8,128)(2,1)} async-done(((bf16[256,4096]{1,0:T(8,128)(2,1)}), bf16[1024,4096]{1,0:T(8,128)(2,1)}) %all-gather.5.cloned.1.call-update) | async-done | bytes 8388624 | tf_op jit(solution)/shard_map/all_gather | solution.py:35
  451.3 11.8 %convert_element_type.48 = f32[1024,4096]{1,0:T(8,128)} convert(bf16[1024,4096]{1,0:T(8,128)(2,1)} %all-gather.5.cloned.1.call-done) | non-fusion elementwise | flops 4194304 | bytes 25165824 | tf_op jit(solution)/shard_map/convert_element_type | solution.py:37
  (69 shorter events, 22.2 us)
Async XLA Ops:
  7.2 154.7 %all-gather.3.cloned.1.call-start = ((), (), s32[]{:S(2)}) async-start(), calls=%async_computation.6 | async-start | bytes 10485760 | tf_op jit(solution)/shard_map/all_gather | solution.py:25
  7.9 169.4 %copy-start.10 = (bf16[1,1024,1024]{2,1,0:T(8,128)(2,1)S(1)}, bf16[1,1024,1024]{2,1,0:T(8,128)(2,1)}, u32[]{:S(2)}) copy-start(bf16[1,1024,1024]{2,1,0:T(8,128)(2,1)} %param.11) | copy-start | bytes 6291460
  7.9 221.9 %reduce-scatter.5.cloned.1.call-start = ((), (), s32[]{:S(2)}) async-start(), calls=%async_computation.7 | async-start | bytes 6291456 | tf_op jit(solution)/shard_map/reduce_scatter | solution.py:38
  177.1 180.4 %reduce-scatter.11.cloned.1.call-start = ((), (), s32[]{:S(2)}) async-start(), calls=%async_computation.10 | async-start | bytes 20971520 | tf_op jit(solution)/shard_map/reduce_scatter | solution.py:34
  192.0 0.7 copy-start.12
  192.0 1.2 copy-start.6
  192.0 2.5 copy-start.7
  197.3 8.3 %copy-start.11 = (s32[1,1024]{1,0:T(1,128)S(1)}, s32[1,1024]{1,0:T(1,128)}, u32[]{:S(2)}) copy-start(s32[1,1024]{1,0:T(1,128)} %param.16) | copy-start | bytes 12292
  201.2 6.3 %copy-start.8 = (bf16[64,8,8,128]{3,2,1,0:T(8,128)(2,1)S(1)}, bf16[64,8,8,128]{3,2,1,0:T(8,128)(2,1)}, u32[]{:S(2)}) copy-start(bf16[64,8,8,128]{3,2,1,0:T(8,128)(2,1)} %copy.77) | copy-start | bytes 3145732
  207.5 9.4 %copy-start.3 = (pred[512,1024]{0,1:T(8,128)(4,1)}, pred[512,1024]{0,1:T(8,128)(4,1)S(1)}, u32[]{:S(2)}) copy-start(pred[512,1024]{0,1:T(8,128)(4,1)S(1)} %fusion.16) | copy-start | bytes 1572868
  216.9 16.1 %copy-start = (f32[64,8,8,128]{3,2,1,0:T(8,128)S(1)}, f32[64,8,8,128]{3,2,1,0:T(8,128)}, u32[]{:S(2)}) copy-start(f32[64,8,8,128]{3,2,1,0:T(8,128)} %copy.79) | copy-start | bytes 6291460
  227.9 6.2 %copy-start.4 = (pred[512,1024]{0,1:T(8,128)(4,1)S(1)}, pred[512,1024]{0,1:T(8,128)(4,1)}, u32[]{:S(2)}) copy-start(pred[512,1024]{0,1:T(8,128)(4,1)} %copy-done.3) | copy-start | bytes 1572868
  233.0 1.0 copy-start.1
  234.1 11.7 %copy-start.9 = (bf16[64,8,8,128]{3,2,1,0:T(8,128)(2,1)S(1)}, bf16[64,8,8,128]{3,2,1,0:T(8,128)(2,1)}, u32[]{:S(2)}) copy-start(bf16[64,8,8,128]{3,2,1,0:T(8,128)(2,1)} %copy.77) | copy-start | bytes 3145732
  245.8 5.7 %copy-start.13 = (bf16[8,512,1024]{1,2,0:T(8,128)(2,1)}, bf16[8,512,1024]{1,2,0:T(8,128)(2,1)S(1)}, u32[]{:S(2)}) copy-start(bf16[8,512,1024]{1,2,0:T(8,128)(2,1)S(1)} %multiply_convert_fusion) | copy-start | bytes 25165828
  251.4 18.1 %all-to-all-start = ((f32[4,256,128]{2,1,0:T(8,128)}), f32[4,256,128]{2,1,0:T(8,128)S(1)}, u32[]{:S(2)}, u32[]{:S(2)}) async-start(f32[4,256,128]{2,1,0:T(8,128)} %bitcast.12), calls=%async_computation.1 | async-start | bytes 1048576 | tf_op jit(solution)/shard_map/all_to_all | solution.py:106
  255.7 118.5 %reduce-scatter.7.cloned.1.call-start = ((), (), s32[]{:S(2)}) async-start(), calls=%async_computation.8 | async-start | bytes 786432 | tf_op jit(solution)/shard_map/reduce_scatter | solution.py:110
  255.7 15.2 %copy-start.2 = (bf16[64,8,8,128]{3,2,1,0:T(8,128)(2,1)S(1)}, bf16[64,8,8,128]{3,2,1,0:T(8,128)(2,1)}, u32[]{:S(2)}) copy-start(bf16[64,8,8,128]{3,2,1,0:T(8,128)(2,1)} %copy-done.1) | copy-start | bytes 3145732
  270.5 120.5 %reduce-scatter.9.cloned.1.call-start = ((), (), s32[]{:S(2)}) async-start(), calls=%async_computation.9 | async-start | bytes 786432 | tf_op jit(solution)/shard_map/reduce_scatter | solution.py:111
  276.8 84.5 %copy-start.5 = (bf16[8,1024,128]{2,1,0:T(8,128)(2,1)S(1)}, bf16[8,1024,128]{2,1,0:T(8,128)(2,1)}, u32[]{:S(2)}) copy-start(bf16[8,1024,128]{2,1,0:T(8,128)(2,1)} %gather_fusion) | copy-start | bytes 6291460
  294.4 156.9 %all-gather.5.cloned.1.call-start = ((), (), s32[]{:S(2)}) async-start(), calls=%async_computation.11 | async-start | bytes 10485760 | tf_op jit(solution)/shard_map/all_gather | solution.py:35
Sparse Core Ops, SparseCore 0:
  9.5 152.3 all-gather.2
  177.2 52.5 reduce-scatter.4
  232.4 125.0 reduce-scatter.10
  359.5 14.6 reduce-scatter.6
  376.3 14.6 reduce-scatter.8
  393.0 58.2 all-gather.4

commit v3 on v2

--- a/solution.py
+++ b/solution.py
@@ -31,10 +31,10 @@
         out_all, dy_block, (((0,), (0,)), ((), ())), preferred_element_type=jnp.float32
     )
     grad_part, weight_part = (grad_part, weight_part)
-    weight_quarter = lax.psum_scatter(weight_part, "dp", scatter_dimension=0, tiled=True)
-    grad_weight = lax.all_gather(
-        weight_quarter.astype(jnp.bfloat16), "dp", axis=0, tiled=True
-    ).astype(jnp.float32)
+    weight_quarter = lax.psum_scatter(
+        weight_part.astype(jnp.bfloat16), "dp", scatter_dimension=0, tiled=True
+    )
+    grad_weight = lax.all_gather(weight_quarter, "dp", axis=0, tiled=True).astype(jnp.float32)
     out_grad = lax.psum_scatter(grad_part, "tsp", scatter_dimension=0, tiled=True).astype(
         jnp.bfloat16
     )

time: 471 us -> 417 us (0.89)
  waiting for transfers between devices: 303 us -> 254 us
    reduce_scatter x1, waiting for transfers between devices: 63 us -> 10.9 us  [per_device(): lax.psum_scatter(weight_part.astype(jnp.bfloat16), 'dp', scatter_dimensio...]
    convert_element_type x2 -> x1, other arithmetic: 15.6 us -> 11.8 us  [per_device(): lax.all_gather(weight_quarter, 'dp', axis=0, tiled=True).astype(jnp.float32)]
    unnamed x36 -> x34, local copies, waits for them, and re-layouts: 11.6 us -> 9.7 us
  transfers between devices with their start and end apart: 7 -> 7, of which waited for: 7 -> 7; matrix products, arithmetic and copies ran while one was open for 21% -> 24% of each run, Pallas kernels for 0% -> 0%
where the time goes in v3:
time: 417 us; the launch traced here: 416 us
  waiting for transfers between devices  254 us (61%)
  matrix products  65.9 us (16%)
  other arithmetic  42.8 us (10%)
  local copies, waits for them, and re-layouts  17.9 us (4%)
  blocking collectives  16.5 us (4%)
  between operations  14.4 us (3%)
  starting transfers between devices  4.98 us (1%)
    all_gather x1, waiting for transfers between devices, per_device(): dy_block = lax.all_gather(grad_out, 'ctx', axis=1, tiled=True)[0]  154 us
    all_gather x1, waiting for transfers between devices, per_device(): lax.all_gather(weight_quarter, 'dp', axis=0, tiled=True).astype(jnp.float32)  58 us
    all_to_all x1, blocking collectives, per_device(): lax.all_to_all(fold_local(value_terms), 'ctx', split_axis=0, concat_axis=...  16.5 us
    dot_general x1, matrix products, per_device(): lax.dot_general(dy_block, out_weight, (((1,), (1,)), ((), ())), preferred...  15.1 us
    reduce_scatter x1, waiting for transfers between devices, per_device(): lax.psum_scatter(fold_remote(value_recv), 'tsp', scatter_dimension=0, til...  15 us
    dot_general x1, matrix products, per_device(): lax.dot_general(out_all, dy_block, (((0,), (0,)), ((), ())), preferred_el...  14.6 us
    convert_element_type x1, other arithmetic, per_device(): lax.all_gather(weight_quarter, 'dp', axis=0, tiled=True).astype(jnp.float32)  11.8 us
    dot_general x1, matrix products, per_device(): jnp.einsum('qhd,khd->hqk', grad_heads, value_heads, preferred_element_typ...  11.7 us
  transfers between devices with their start and end apart: 7, of which 7 were waited for; matrix products, arithmetic and copies ran while one was open for 24% of the time, Pallas kernels for 0%

profile of v3, /device:TPU:0, one launch (start us, length us, event | category | flops | bytes accessed | tf_op | source)
XLA Modules:
  0.0 416.2 jit_solution(13732216424792096202)
XLA Ops:
  8.0 154.0 %all-gather.3.cloned.1.call-done = bf16[1,1024,4096]{2,1,0:T(8,128)(2,1)} async-done(((bf16[1,256,4096]{2,1,0:T(8,128)(2,1)}), bf16[1,1024,4096]{2,1,0:T(8,128)(2,1)}) %all-gather.3.cloned.1.call-update) | async-done | bytes 8388624 | tf_op jit(solution)/shard_map/all_gather | solution.py:25
  161.9 15.1 %fusion.6 = f32[1024,1024]{1,0:T(8,128)} fusion(bf16[1024,4096]{1,0:T(8,128)(2,1)} %param.12, bf16[1,1024,4096]{2,1,0:T(8,128)(2,1)} %all-gather.3.cloned.1.call-done), kind=kOutput, calls=%fused_computation.12 | convolution fusion | flops 8589934592 | bytes 20971520 | tf_op jit(solution)/shard_map/dot_general | solution.py:26
  177.2 14.6 %fusion.8 = bf16[1024,4096]{1,0:T(8,128)(2,1)} fusion(bf16[1,1024,4096]{2,1,0:T(8,128)(2,1)} %all-gather.3.cloned.1.call-done, bf16[1,1024,1024]{2,1,0:T(8,128)(2,1)S(1)} %copy-done.9), kind=kOutput, calls=%fused_computation.14 | convolution fusion | flops 8594128896 | bytes 18874368 | tf_op jit(solution)/shard_map/dot_general | solution.py:30
  195.5 1.6 convert_bitcast_fusion
  197.1 1.8 copy.79
  201.1 2.2 gather_fusion
  203.3 2.2 gather_fusion.1
  207.5 9.4 %fusion.3 = (f32[8,512]{1,0:T(8,128)S(1)}, f32[8,1024,512]{2,1,0:T(8,128)}) fusion(pred[512,1024]{0,1:T(8,128)(4,1)S(1)} %fusion.19, bf16[512,8,128]{2,1,0:T(8,128)(2,1)S(1)} %bitcast.109, bf16[8,1024,128]{2,1,0:T(8,128)(2,1)} %gather_fusion, pred[8]{0:T(512)(128)(4,1)S(1)} %compare_and_fusion), kind=kOutput, calls=%fused_computation.9 | convolution fusion | flops 1087369216 | bytes 20463624 | tf_op jit(solution)/shard_map/qhd,khd->hqk/dot_general | solution.py:71
  216.9 9.4 %exponential_reduce_fusion = f32[8,512]{1,0:T(8,128)S(1)} fusion(f32[8,1024,512]{2,1,0:T(8,128)} %get-tuple-element.24, f32[8,512]{1,0:T(8,128)S(1)} %get-tuple-element.23, pred[512,1024]{0,1:T(8,128)(4,1)S(1)} %fusion.19), kind=kLoop, calls=%fused_computation.8 | loop fusion | flops 16773120 | bytes 17334272 | tf_op jit(solution)/shard_map/reduce_sum | solution.py:76
  227.9 1.9 reduce-scatter.5.cloned.1.call-done
  229.7 2.9 convert_bitcast_fusion.1
  234.1 11.7 %multiply_convert_fusion = bf16[8,512,1024]{1,2,0:T(8,128)(2,1)S(1)} fusion(f32[8,1024,512]{2,1,0:T(8,128)} %get-tuple-element.24, f32[8,512]{1,0:T(8,128)S(1)} %copy.58, f32[8,512]{1,0:T(8,128)S(1)} %log_add_fusion, pred[512,1024]{0,1:T(8,128)(4,1)S(1)} %copy-done.4, bf16[8,1024,128]{2,1,0:T(8,128)(2,1)} %gather_fusion.1, ...), kind=kOutput, calls=%fused_computation.7 | convolution fusion | flops 1104150528 | bytes 28868616 | tf_op jit(solution)/shard_map/qhd,khd->hqk/dot_general | solution.py:82
  245.8 3.5 multiply_reduce_fusion
  249.3 4.3 %all-to-all-start = ((f32[4,256,128]{2,1,0:T(8,128)}), f32[4,256,128]{2,1,0:T(8,128)S(1)}, u32[]{:S(2)}, u32[]{:S(2)}) async-start(f32[4,256,128]{2,1,0:T(8,128)} %bitcast.12), calls=%async_computation.1 | async-start | bytes 1048576 | tf_op jit(solution)/shard_map/all_to_all | solution.py:106
  253.7 11.3 %fusion.2 = bf16[1024,512,8]{1,0,2:T(8,128)(2,1)} fusion(f32[8,1024,512]{2,1,0:T(8,128)} %get-tuple-element.24, f32[512,8]{0,1:T(8,128)S(1)} %bitcast.113, pred[1024,512]{1,0:T(8,128)(4,1)S(1)} %fusion.43), kind=kLoop, calls=%fused_computation.5 | loop fusion | flops 20971520 | bytes 25706496 | tf_op jit(solution)/shard_map/convert_element_type | solution.py:78
  265.0 3.0 all-to-all-done
  269.4 6.0 %convolution_bitcast_fusion = f32[4,256,128]{2,1,0:T(8,128)S(1)} fusion(bf16[4,256,512,8]{2,1,0,3:T(8,128)(2,1)} %bitcast.97, bf16[512,8,128,1]{2,1,0,3:T(8,128)(2,1)S(1)} %bitcast.101), kind=kOutput, calls=%fused_computation.32 | convolution fusion | flops 1073741824 | bytes 9961472 | tf_op jit(solution)/shard_map/hqk,qhd->hkd/dot_general | solution.py:79
  275.3 16.5 %all_to_all.29 = f32[4,256,128]{2,1,0:T(8,128)S(1)} all-to-all(f32[4,256,128]{2,1,0:T(8,128)S(1)} %convolution_bitcast_fusion), channel_id=1, replica_groups=mesh['dp'=4,'ctx'=4,'tsp'=2] {'ctx'}, dimensions={0} | all-to-all | bytes 1048576 | tf_op jit(solution)/shard_map/all_to_all | solution.py:107
  292.9 10.9 %reduce-scatter.11.cloned.1.call-done = bf16[256,4096]{1,0:T(8,128)(2,1)} async-done(((bf16[1024,4096]{1,0:T(8,128)(2,1)}), bf16[256,4096]{1,0:T(8,128)(2,1)}) %reduce-scatter.11.cloned.1.call-update) | async-done | bytes 2097168 | tf_op jit(solution)/shard_map/reduce_scatter | solution.py:34
  303.8 5.6 %multiply_convert_fusion.1 = bf16[8,128,512]{2,1,0:T(8,128)(2,1)S(1)} fusion(bf16[8,512,1024]{1,2,0:T(8,128)(2,1)} %copy-done.12, bf16[8,1024,128]{2,1,0:T(8,128)(2,1)} %gather_fusion, pred[8]{0:T(512)(128)(4,1)S(1)} %compare_and_fusion), kind=kOutput, calls=%fused_computation.24 | convolution fusion | flops 1075838976 | bytes 11534344 | tf_op jit(solution)/shard_map/hqk,khd->qhd/dot_general | solution.py:88
  310.7 10.3 %reduce-scatter.7.cloned.1.call-done = f32[128,512]{0,1:T(8,128)} async-done(((f32[256,512]{0,1:T(8,128)}), f32[128,512]{0,1:T(8,128)}) %reduce-scatter.7.cloned.1.call-update) | async-done | bytes 262160 | tf_op jit(solution)/shard_map/reduce_scatter | solution.py:110
  322.8 15.0 %reduce-scatter.9.cloned.1.call-done = f32[128,512]{0,1:T(8,128)} async-done(((f32[256,512]{0,1:T(8,128)}), f32[128,512]{0,1:T(8,128)}) %reduce-scatter.9.cloned.1.call-update) | async-done | bytes 262160 | tf_op jit(solution)/shard_map/reduce_scatter | solution.py:111
  339.5 58.0 %all-gather.5.cloned.1.call-done = bf16[1024,4096]{1,0:T(8,128)(2,1)} async-done(((bf16[256,4096]{1,0:T(8,128)(2,1)}), bf16[1024,4096]{1,0:T(8,128)(2,1)}) %all-gather.5.cloned.1.call-update) | async-done | bytes 8388624 | tf_op jit(solution)/shard_map/all_gather | solution.py:37
  397.5 11.8 %convert_element_type.48 = f32[1024,4096]{1,0:T(8,128)} convert(bf16[1024,4096]{1,0:T(8,128)(2,1)} %all-gather.5.cloned.1.call-done) | non-fusion elementwise | flops 4194304 | bytes 25165824 | tf_op jit(solution)/shard_map/convert_element_type | solution.py:37
  (66 shorter events, 18.9 us)
Async XLA Ops:
  7.2 154.7 %all-gather.3.cloned.1.call-start = ((), (), s32[]{:S(2)}) async-start(), calls=%async_computation.6 | async-start | bytes 10485760 | tf_op jit(solution)/shard_map/all_gather | solution.py:25
  7.9 169.3 %copy-start.9 = (bf16[1,1024,1024]{2,1,0:T(8,128)(2,1)S(1)}, bf16[1,1024,1024]{2,1,0:T(8,128)(2,1)}, u32[]{:S(2)}) copy-start(bf16[1,1024,1024]{2,1,0:T(8,128)(2,1)} %param.11) | copy-start | bytes 6291460
  7.9 221.8 %reduce-scatter.5.cloned.1.call-start = ((), (), s32[]{:S(2)}) async-start(), calls=%async_computation.7 | async-start | bytes 6291456 | tf_op jit(solution)/shard_map/reduce_scatter | solution.py:38
  177.0 126.7 %reduce-scatter.11.cloned.1.call-start = ((), (), s32[]{:S(2)}) async-start(), calls=%async_computation.10 | async-start | bytes 10485760 | tf_op jit(solution)/shard_map/reduce_scatter | solution.py:34
  191.8 0.7 copy-start.11
  191.8 1.2 copy-start.5
  191.8 2.5 copy-start.6
  197.1 8.4 %copy-start.10 = (s32[1,1024]{1,0:T(1,128)S(1)}, s32[1,1024]{1,0:T(1,128)}, u32[]{:S(2)}) copy-start(s32[1,1024]{1,0:T(1,128)} %param.16) | copy-start | bytes 12292
  201.1 6.4 %copy-start.7 = (bf16[64,8,8,128]{3,2,1,0:T(8,128)(2,1)S(1)}, bf16[64,8,8,128]{3,2,1,0:T(8,128)(2,1)}, u32[]{:S(2)}) copy-start(bf16[64,8,8,128]{3,2,1,0:T(8,128)(2,1)} %copy.77) | copy-start | bytes 3145732
  207.4 9.4 %copy-start.3 = (pred[512,1024]{0,1:T(8,128)(4,1)}, pred[512,1024]{0,1:T(8,128)(4,1)S(1)}, u32[]{:S(2)}) copy-start(pred[512,1024]{0,1:T(8,128)(4,1)S(1)} %fusion.19) | copy-start | bytes 1572868
  216.9 16.0 %copy-start = (f32[64,8,8,128]{3,2,1,0:T(8,128)S(1)}, f32[64,8,8,128]{3,2,1,0:T(8,128)}, u32[]{:S(2)}) copy-start(f32[64,8,8,128]{3,2,1,0:T(8,128)} %copy.79) | copy-start | bytes 6291460
  227.9 6.2 %copy-start.4 = (pred[512,1024]{0,1:T(8,128)(4,1)S(1)}, pred[512,1024]{0,1:T(8,128)(4,1)}, u32[]{:S(2)}) copy-start(pred[512,1024]{0,1:T(8,128)(4,1)} %copy-done.3) | copy-start | bytes 1572868
  232.9 1.0 copy-start.1
  234.0 11.7 %copy-start.8 = (bf16[64,8,8,128]{3,2,1,0:T(8,128)(2,1)S(1)}, bf16[64,8,8,128]{3,2,1,0:T(8,128)(2,1)}, u32[]{:S(2)}) copy-start(bf16[64,8,8,128]{3,2,1,0:T(8,128)(2,1)} %copy.77) | copy-start | bytes 3145732
  245.8 3.6 copy-start.12
  249.3 18.7 %all-to-all-start = ((f32[4,256,128]{2,1,0:T(8,128)}), f32[4,256,128]{2,1,0:T(8,128)S(1)}, u32[]{:S(2)}, u32[]{:S(2)}) async-start(f32[4,256,128]{2,1,0:T(8,128)} %bitcast.12), calls=%async_computation.1 | async-start | bytes 1048576 | tf_op jit(solution)/shard_map/all_to_all | solution.py:106
  253.7 67.4 %reduce-scatter.7.cloned.1.call-start = ((), (), s32[]{:S(2)}) async-start(), calls=%async_computation.8 | async-start | bytes 786432 | tf_op jit(solution)/shard_map/reduce_scatter | solution.py:110
  253.7 15.7 %copy-start.2 = (bf16[64,8,8,128]{3,2,1,0:T(8,128)(2,1)S(1)}, bf16[64,8,8,128]{3,2,1,0:T(8,128)(2,1)}, u32[]{:S(2)}) copy-start(bf16[64,8,8,128]{3,2,1,0:T(8,128)(2,1)} %copy-done.1) | copy-start | bytes 3145732
  269.0 68.8 %reduce-scatter.9.cloned.1.call-start = ((), (), s32[]{:S(2)}) async-start(), calls=%async_computation.9 | async-start | bytes 786432 | tf_op jit(solution)/shard_map/reduce_scatter | solution.py:111
  292.8 104.7 %all-gather.5.cloned.1.call-start = ((), (), s32[]{:S(2)}) async-start(), calls=%async_computation.11 | async-start | bytes 10485760 | tf_op jit(solution)/shard_map/all_gather | solution.py:37
Sparse Core Ops, SparseCore 0:
  9.5 152.3 all-gather.2
  177.1 52.5 reduce-scatter.4
  232.3 71.3 reduce-scatter.10
  306.4 14.6 reduce-scatter.6
  323.1 14.6 reduce-scatter.8
  339.2 58.2 all-gather.4

commit v4 on v3

--- a/solution.py
+++ b/solution.py
@@ -22,19 +22,27 @@
     out_all = attn_out[0]
     seq_len = out_all.shape[0]
     feat_width = out_all.shape[1]
-    dy_block = lax.all_gather(grad_out, "ctx", axis=1, tiled=True)[0]
-    proj_rows = lax.dot_general(
-        dy_block, out_weight, (((1,), (1,)), ((), ())), preferred_element_type=jnp.float32
-    )
+    dy_local = grad_out[0]
+    chunk_width = dy_local.shape[1] // 2
+    proj_rows = None
+    weight_cols = []
+    for chunk_index in range(2):
+        chunk_cols = slice(chunk_index * chunk_width, (chunk_index + 1) * chunk_width)
+        dy_chunk = lax.all_gather(dy_local[:, chunk_cols], "ctx", axis=0, tiled=True)
+        proj_chunk = lax.dot_general(
+            dy_chunk, out_weight[:, chunk_cols], (((1,), (1,)), ((), ())),
+            preferred_element_type=jnp.float32,
+        )
+        proj_rows = proj_chunk if proj_rows is None else proj_rows + proj_chunk
+        weight_chunk = lax.dot_general(
+            out_all, dy_chunk, (((0,), (0,)), ((), ())), preferred_element_type=jnp.float32
+        )
+        weight_quarter = lax.psum_scatter(
+            weight_chunk.astype(jnp.bfloat16), "dp", scatter_dimension=0, tiled=True
+        )
+        weight_cols.append(lax.all_gather(weight_quarter, "dp", axis=0, tiled=True))
+    grad_weight = jnp.concatenate(weight_cols, axis=1).astype(jnp.float32)
     grad_part = proj_rows
-    weight_part = lax.dot_general(
-        out_all, dy_block, (((0,), (0,)), ((), ())), preferred_element_type=jnp.float32
-    )
-    grad_part, weight_part = (grad_part, weight_part)
-    weight_quarter = lax.psum_scatter(
-        weight_part.astype(jnp.bfloat16), "dp", scatter_dimension=0, tiled=True
-    )
-    grad_weight = lax.all_gather(weight_quarter, "dp", axis=0, tiled=True).astype(jnp.float32)
     out_grad = lax.psum_scatter(grad_part, "tsp", scatter_dimension=0, tiled=True).astype(
         jnp.bfloat16
     )

time: 417 us -> 459 us (1.10)
  waiting for transfers between devices: 254 us -> 282 us
  matrix products: 65.9 us -> 74.2 us
  local copies, waits for them, and re-layouts: 17.9 us -> 25.2 us
    reduce_scatter x1 -> x2, waiting for transfers between devices: 10.9 us -> 26 us  [per_device(): lax.psum_scatter(weight_chunk.astype(jnp.bfloat16), 'dp', scatter_dimensi...]
    all_gather x2 -> x4, waiting for transfers between devices: 212 us -> 225 us  [the longest x2 154 us: per_device(): lax.all_gather(dy_local[:, chunk_cols], 'ctx', axis=0, tiled=True)]
    dot_general x2 -> x4, matrix products: 29.6 us -> 39 us  [the longest x2 21.2 us: per_device(): lax.dot_general(dy_chunk, out_weight[:, chunk_cols], (((1,), (1,)), ((),...]
  transfers between devices with their start and end apart: 7 -> 10, of which waited for: 7 -> 8; matrix products, arithmetic and copies ran while one was open for 24% -> 25% of each run, Pallas kernels for 0% -> 0%
where the time goes in v4:
time: 459 us; the launch traced here: 458 us
  waiting for transfers between devices  282 us (61%)
  matrix products  74.2 us (16%)
  other arithmetic  42.1 us (9%)
  local copies, waits for them, and re-layouts  25.2 us (5%)
  blocking collectives  16.6 us (4%)
  between operations  14.2 us (3%)
    all_gather x2, waiting for transfers between devices, per_device(): lax.all_gather(dy_local[:, chunk_cols], 'ctx', axis=0, tiled=True)  154 us
    all_gather x2, waiting for transfers between devices, per_device(): weight_cols.append(lax.all_gather(weight_quarter, 'dp', axis=0, tiled=True))  70.4 us
    reduce_scatter x2, waiting for transfers between devices, per_device(): lax.psum_scatter(weight_chunk.astype(jnp.bfloat16), 'dp', scatter_dimensi...  26 us
    dot_general x2, matrix products, per_device(): lax.dot_general(dy_chunk, out_weight[:, chunk_cols], (((1,), (1,)), ((),...  21.2 us
    dot_general x2, matrix products, per_device(): lax.dot_general(out_all, dy_chunk, (((0,), (0,)), ((), ())), preferred_el...  17.8 us
    all_to_all x1, blocking collectives, per_device(): lax.all_to_all(fold_local(value_terms), 'ctx', split_axis=0, concat_axis=...  16.6 us
    reduce_scatter x1, waiting for transfers between devices, per_device(): lax.psum_scatter(fold_remote(value_recv), 'tsp', scatter_dimension=0, til...  15.2 us
    unnamed x34, local copies, waits for them, and re-layouts  12.9 us
  transfers between devices with their start and end apart: 10, of which 8 were waited for; matrix products, arithmetic and copies ran while one was open for 25% of the time, Pallas kernels for 0%

profile of v4, /device:TPU:0, one launch (start us, length us, event | category | flops | bytes accessed | tf_op | source)
XLA Modules:
  0.0 458.3 jit_solution(17889082660179477620)
XLA Ops:
  7.2 3.1 fusion.40
  11.1 82.8 %all-gather.7.cloned.1.call-done = bf16[1024,2048]{1,0:T(8,128)(2,1)} async-done(((bf16[256,2048]{1,0:T(8,128)(2,1)}), bf16[1024,2048]{1,0:T(8,128)(2,1)}) %all-gather.7.cloned.1.call-update) | async-done | bytes 4194320 | tf_op jit(solution)/shard_map/all_gather | solution.py:31
  94.0 10.0 %fusion.4 = f32[1024,1024]{1,0:T(8,128)} fusion(bf16[1024,2048]{1,0:T(8,128)(2,1)} %all-gather.7.cloned.1.call-done, bf16[1024,4096]{1,0:T(8,128)(2,1)} %param.12), kind=kOutput, calls=%fused_computation.12 | convolution fusion | flops 4294967296 | bytes 12582912 | tf_op jit(solution)/shard_map/dot_general | solution.py:32
  104.0 71.4 %all-gather.5.cloned.1.call-done = bf16[1024,2048]{1,0:T(8,128)(2,1)} async-done(((bf16[256,2048]{1,0:T(8,128)(2,1)}), bf16[1024,2048]{1,0:T(8,128)(2,1)}) %all-gather.5.cloned.1.call-update) | async-done | bytes 4194320 | tf_op jit(solution)/shard_map/all_gather | solution.py:31
  175.4 11.2 %fusion.19 = f32[1024,1024]{1,0:T(8,128)} fusion(f32[1024,1024]{1,0:T(8,128)} %fusion.4, bf16[1024,2048]{1,0:T(8,128)(2,1)} %all-gather.5.cloned.1.call-done, bf16[1024,4096]{1,0:T(8,128)(2,1)} %param.12), kind=kOutput, calls=%fused_computation.35 | convolution fusion | flops 4296015872 | bytes 16777216 | tf_op jit(solution)/shard_map/dot_general | solution.py:32
  188.1 8.3 %convolution_convert_fusion = bf16[1024,2048]{1,0:T(8,128)(2,1)} fusion(bf16[1024,2048]{1,0:T(8,128)(2,1)} %all-gather.7.cloned.1.call-done, bf16[1,1024,1024]{2,1,0:T(8,128)(2,1)S(1)} %copy-done.9), kind=kOutput, calls=%fused_computation.16 | convolution fusion | flops 4297064448 | bytes 10485760 | tf_op jit(solution)/shard_map/dot_general | solution.py:37
  198.2 9.5 %convolution_convert_fusion.1 = bf16[1024,2048]{1,0:T(8,128)(2,1)} fusion(bf16[1024,2048]{1,0:T(8,128)(2,1)} %all-gather.5.cloned.1.call-done, bf16[1,1024,1024]{2,1,0:T(8,128)(2,1)} %param.11), kind=kOutput, calls=%fused_computation.17 | convolution fusion | flops 4297064448 | bytes 10485760 | tf_op jit(solution)/shard_map/dot_general | solution.py:37
  224.4 9.3 %fusion.3 = (f32[8,512]{1,0:T(8,128)S(1)}, f32[8,1024,512]{2,1,0:T(8,128)}) fusion(pred[512,1024]{0,1:T(8,128)(4,1)S(1)} %fusion.17, bf16[512,8,128]{2,1,0:T(8,128)(2,1)} %bitcast.109, bf16[8,1024,128]{2,1,0:T(8,128)(2,1)S(1)} %copy-done.5, pred[8]{0:T(512)(128)(4,1)S(1)} %compare_and_fusion), kind=kOutput, calls=%fused_computation.9 | convolution fusion | flops 1087369216 | bytes 20463624 | tf_op jit(solution)/shard_map/qhd,khd->hqk/dot_general | solution.py:79
  233.7 9.2 %exponential_reduce_fusion = f32[8,512]{1,0:T(8,128)S(1)} fusion(f32[8,1024,512]{2,1,0:T(8,128)} %get-tuple-element.26, f32[8,512]{1,0:T(8,128)S(1)} %get-tuple-element.25, pred[512,1024]{0,1:T(8,128)(4,1)S(1)} %fusion.17), kind=kLoop, calls=%fused_computation.8 | loop fusion | flops 16773120 | bytes 17334272 | tf_op jit(solution)/shard_map/reduce_sum | solution.py:84
  244.5 3.0 convert_bitcast_fusion.1
  248.9 11.7 %multiply_convert_fusion = bf16[8,512,1024]{1,2,0:T(8,128)(2,1)S(1)} fusion(f32[8,1024,512]{2,1,0:T(8,128)} %get-tuple-element.26, f32[8,512]{1,0:T(8,128)S(1)} %copy.58, f32[8,512]{1,0:T(8,128)S(1)} %log_add_fusion, pred[512,1024]{0,1:T(8,128)(4,1)S(1)} %copy-done.4, bf16[8,1024,128]{2,1,0:T(8,128)(2,1)} %gather_fusion.1, ...), kind=kOutput, calls=%fused_computation.7 | convolution fusion | flops 1104150528 | bytes 28868616 | tf_op jit(solution)/shard_map/qhd,khd->hqk/dot_general | solution.py:90
  260.6 3.5 multiply_reduce_fusion
  264.1 3.5 all-to-all-start
  267.7 10.8 %fusion.2 = bf16[1024,512,8]{1,0,2:T(8,128)(2,1)} fusion(f32[8,1024,512]{2,1,0:T(8,128)} %get-tuple-element.26, f32[512,8]{0,1:T(8,128)S(1)} %bitcast.113, pred[1024,512]{1,0:T(8,128)(4,1)S(1)} %fusion.48), kind=kLoop, calls=%fused_computation.5 | loop fusion | flops 20971520 | bytes 25706496 | tf_op jit(solution)/shard_map/convert_element_type | solution.py:86
  278.5 3.8 all-to-all-done
  283.4 5.7 %convolution_bitcast_fusion = f32[4,256,128]{2,1,0:T(8,128)S(1)} fusion(bf16[4,256,512,8]{2,1,0,3:T(8,128)(2,1)} %bitcast.96, bf16[512,8,128,1]{2,1,0,3:T(8,128)(2,1)S(1)} %bitcast.100), kind=kOutput, calls=%fused_computation.36 | convolution fusion | flops 1073741824 | bytes 9961472 | tf_op jit(solution)/shard_map/hqk,qhd->hkd/dot_general | solution.py:87
  289.1 16.6 %all_to_all.29 = f32[4,256,128]{2,1,0:T(8,128)S(1)} all-to-all(f32[4,256,128]{2,1,0:T(8,128)S(1)} %convolution_bitcast_fusion), channel_id=1, replica_groups=mesh['dp'=4,'ctx'=4,'tsp'=2] {'ctx'}, dimensions={0} | all-to-all | bytes 1048576 | tf_op jit(solution)/shard_map/all_to_all | solution.py:115
  307.5 26.0 %reduce-scatter.12.cloned.1.call-done = bf16[256,2048]{1,0:T(8,128)(2,1)} async-done(((bf16[1024,2048]{1,0:T(8,128)(2,1)}), bf16[256,2048]{1,0:T(8,128)(2,1)}) %reduce-scatter.12.cloned.1.call-update) | async-done | bytes 1048592 | tf_op jit(solution)/shard_map/reduce_scatter | solution.py:40
  333.6 5.0 %multiply_convert_fusion.1 = bf16[8,128,512]{2,1,0:T(8,128)(2,1)S(1)} fusion(bf16[8,512,1024]{1,2,0:T(8,128)(2,1)} %copy-done.12, bf16[8,1024,128]{2,1,0:T(8,128)(2,1)S(1)} %copy-done.6, pred[8]{0:T(512)(128)(4,1)S(1)} %compare_and_fusion), kind=kOutput, calls=%fused_computation.27 | convolution fusion | flops 1075838976 | bytes 11534344 | tf_op jit(solution)/shard_map/hqk,khd->qhd/dot_general | solution.py:96
  339.9 11.0 %reduce-scatter.8.cloned.1.call-done = f32[128,512]{0,1:T(8,128)} async-done(((f32[256,512]{0,1:T(8,128)}), f32[128,512]{0,1:T(8,128)}) %reduce-scatter.8.cloned.1.call-update) | async-done | bytes 262160 | tf_op jit(solution)/shard_map/reduce_scatter | solution.py:118
  352.6 15.2 %reduce-scatter.10.cloned.1.call-done = f32[128,512]{0,1:T(8,128)} async-done(((f32[256,512]{0,1:T(8,128)}), f32[128,512]{0,1:T(8,128)}) %reduce-scatter.10.cloned.1.call-update) | async-done | bytes 262160 | tf_op jit(solution)/shard_map/reduce_scatter | solution.py:119
  369.5 34.3 %all-gather.11.cloned.1.call-done = bf16[1024,2048]{1,0:T(8,128)(2,1)} async-done(((bf16[256,2048]{1,0:T(8,128)(2,1)}), bf16[1024,2048]{1,0:T(8,128)(2,1)}) %all-gather.11.cloned.1.call-update) | async-done | bytes 4194320 | tf_op jit(solution)/shard_map/all_gather | solution.py:43
  403.8 36.1 %all-gather.9.cloned.1.call-done = bf16[1024,2048]{1,0:T(8,128)(2,1)} async-done(((bf16[256,2048]{1,0:T(8,128)(2,1)}), bf16[1024,2048]{1,0:T(8,128)(2,1)}) %all-gather.9.cloned.1.call-update) | async-done | bytes 4194320 | tf_op jit(solution)/shard_map/all_gather | solution.py:43
  439.9 11.9 %maximum_convert_fusion = f32[1024,4096]{1,0:T(8,128)} fusion(bf16[1024,2048]{1,0:T(8,128)(2,1)} %all-gather.11.cloned.1.call-done, bf16[1024,2048]{1,0:T(8,128)(2,1)} %all-gather.9.cloned.1.call-done), kind=kLoop, calls=%fused_computation.10 | loop fusion | flops 16777216 | bytes 25165824 | tf_op jit(solution)/shard_map/convert_element_type | solution.py:44
  (78 shorter events, 31.4 us)
Async XLA Ops:
  7.2 86.8 %all-gather.7.cloned.1.call-start = ((), (), s32[]{:S(2)}) async-start(), calls=%async_computation.8 | async-start | bytes 5242880 | tf_op jit(solution)/shard_map/all_gather | solution.py:31
  10.3 165.0 %all-gather.5.cloned.1.call-start = ((), (), s32[]{:S(2)}) async-start(), calls=%async_computation.7 | async-start | bytes 5242880 | tf_op jit(solution)/shard_map/all_gather | solution.py:31
  11.1 233.4 %reduce-scatter.6.cloned.1.call-start = ((), (), s32[]{:S(2)}) async-start(), calls=%async_computation.9 | async-start | bytes 6291456 | tf_op jit(solution)/shard_map/reduce_scatter | solution.py:46
  186.5 1.6 copy-start.9
  186.5 120.3 %reduce-scatter.14.cloned.1.call-start = ((), (), s32[]{:S(2)}) async-start(), calls=%async_computation.14 | async-start | bytes 5242880 | tf_op jit(solution)/shard_map/reduce_scatter | solution.py:40
  196.4 137.1 %reduce-scatter.12.cloned.1.call-start = ((), (), s32[]{:S(2)}) async-start(), calls=%async_computation.12 | async-start | bytes 5242880 | tf_op jit(solution)/shard_map/reduce_scatter | solution.py:40
  207.7 0.7 copy-start.11
  207.7 1.2 copy-start.7
  218.0 4.4 copy-start.10
  220.2 4.2 copy-start.5
  224.4 9.3 %copy-start.3 = (pred[512,1024]{0,1:T(8,128)(4,1)}, pred[512,1024]{0,1:T(8,128)(4,1)S(1)}, u32[]{:S(2)}) copy-start(pred[512,1024]{0,1:T(8,128)(4,1)S(1)} %fusion.17) | copy-start | bytes 1572868
  242.9 4.9 %copy-start = (f32[64,8,8,128]{3,2,1,0:T(8,128)S(1)}, f32[64,8,8,128]{3,2,1,0:T(8,128)}, u32[]{:S(2)}) copy-start(f32[64,8,8,128]{3,2,1,0:T(8,128)} %copy.79) | copy-start | bytes 6291460
  244.5 4.4 copy-start.4
  247.8 1.1 copy-start.1
  248.9 11.7 %copy-start.8 = (bf16[64,8,8,128]{3,2,1,0:T(8,128)(2,1)S(1)}, bf16[64,8,8,128]{3,2,1,0:T(8,128)(2,1)}, u32[]{:S(2)}) copy-start(bf16[64,8,8,128]{3,2,1,0:T(8,128)(2,1)} %copy.77) | copy-start | bytes 3145732
  260.6 3.6 copy-start.12
  264.1 18.1 %all-to-all-start = ((f32[4,256,128]{2,1,0:T(8,128)}), f32[4,256,128]{2,1,0:T(8,128)S(1)}, u32[]{:S(2)}, u32[]{:S(2)}) async-start(f32[4,256,128]{2,1,0:T(8,128)} %bitcast.12), calls=%async_computation.1 | async-start | bytes 1048576 | tf_op jit(solution)/shard_map/all_to_all | solution.py:114
  267.6 83.3 %reduce-scatter.8.cloned.1.call-start = ((), (), s32[]{:S(2)}) async-start(), calls=%async_computation.10 | async-start | bytes 786432 | tf_op jit(solution)/shard_map/reduce_scatter | solution.py:118
  267.7 15.7 %copy-start.2 = (bf16[64,8,8,128]{3,2,1,0:T(8,128)(2,1)S(1)}, bf16[64,8,8,128]{3,2,1,0:T(8,128)(2,1)}, u32[]{:S(2)}) copy-start(bf16[64,8,8,128]{3,2,1,0:T(8,128)(2,1)} %copy-done.1) | copy-start | bytes 3145732
  283.3 84.5 %reduce-scatter.10.cloned.1.call-start = ((), (), s32[]{:S(2)}) async-start(), calls=%async_computation.11 | async-start | bytes 786432 | tf_op jit(solution)/shard_map/reduce_scatter | solution.py:119
  289.1 44.5 %copy-start.6 = (bf16[8,1024,128]{2,1,0:T(8,128)(2,1)S(1)}, bf16[8,1024,128]{2,1,0:T(8,128)(2,1)}, u32[]{:S(2)}) copy-start(bf16[8,1024,128]{2,1,0:T(8,128)(2,1)} %gather_fusion) | copy-start | bytes 6291460
  306.7 97.1 %all-gather.11.cloned.1.call-start = ((), (), s32[]{:S(2)}) async-start(), calls=%async_computation.15 | async-start | bytes 5242880 | tf_op jit(solution)/shard_map/all_gather | solution.py:43
  307.5 132.4 %all-gather.9.cloned.1.call-start = ((), (), s32[]{:S(2)}) async-start(), calls=%async_computation.13 | async-start | bytes 5242880 | tf_op jit(solution)/shard_map/all_gather | solution.py:43
Sparse Core Ops, SparseCore 0:
  10.5 83.4 all-gather.6
  96.1 79.2 all-gather.4
  186.7 52.8 reduce-scatter.5
  241.9 44.5 reduce-scatter.13
  288.9 44.5 reduce-scatter.11
  336.2 14.6 reduce-scatter.7
  353.1 14.6 reduce-scatter.9
  369.3 34.4 all-gather.10
  405.4 34.4 all-gather.8
